TPU v7x, 128 devices: a whole 4x4x4 slice. The times are simulated.
128 devices in a mesh: blk: 32 (over x, z, core), tok: 4 (over y).
Axes of the slice: x: 4, y: 4, z: 4, core: 2. Of those that a mesh axis runs over, the one named last changes fastest.
Arguments:
- stream: bfloat16 [16384, 1664], P(('tok', 'blk'))
- queries: bfloat16 [16384, 1664], P(('tok', 'blk'))
- key_cache: bfloat16 [16384, 1664], P(('tok', 'blk'))
- value_cache: bfloat16 [16384, 1664], P(('tok', 'blk')), may hold values from -6 to 6
- segments: int32 [16384], P('tok'), may hold values from 63 to 16383, as said below
- stale_rows: int32 [1536], P(('tok', 'blk')), may hold values from 0 to 16383, as said below
- owners: int32 [4096], P(('tok', 'blk')), may hold values from 0 to 3, as said below
- attn_gain: float32 [1664], replicated, may hold values from 0.1 to 1.9
- w_key: bfloat16 [1664, 1664], replicated, may hold values from -0.15625 to 0.15625
- key_bias: float32 [1664], replicated, may hold values from -3 to 3
- mlp_gain: float32 [1664], replicated, may hold values from 0.1 to 1.9
- w_fc: bfloat16 [1664, 8192], P(None, 'blk'), may hold values from -0.15625 to 0.15625
- b_fc: float32 [8192], P('blk'), may hold values from -3 to 3
- w_proj: bfloat16 [8192, 1664], P('blk'), may hold values from -0.125 to 0.125
- b_proj: float32 [1664], replicated, may hold values from -3 to 3
- merge_gain: float32 [1664], replicated, may hold values from 0.1 to 1.9
- w_merge: bfloat16 [1664, 1664], replicated, may hold values from -0.15625 to 0.15625
- b_merge: float32 [1664], replicated, may hold values from -3 to 3
Outputs:
- refreshed_keys: bfloat16 [16384, 1664], P(('tok', 'blk'))
- delivered: bfloat16 [4, 32, 128, 1664], P('tok', 'blk')
Inputs may be any that keep to these rules, and one draw needn't show every extreme that they name: `segments`: A segment's id is the index of its last row, so ids never fall; each segment has 4 to 128 rows, a multiple of 4, and lies inside one aligned block of 4096 rows; each such block begins with a segment of 64 rows followed by one of exactly 128 rows. `stale_rows`: Distinct; the aligned block of 128 rows of each device holds exactly 12 of them, all inside that block and listed on that device; row 0 and the last row are always listed. `owners`: all merged tokens of one segment (the segment of row 4 m for merged token m) have the same owner.
All inputs are finite; a program needn't handle non-finite values.
Results may differ from a plain program's by a relative error of at most 0.011.
Values may be sent and summed in bfloat16 or wider, within the bound.
No kernel may reach another device: no remote copies, remote signals or barrier semaphores. Data moves between devices by JAX's collectives and lax.ppermute only.
A program may use at most 192 MiB of HBM per device.

v0:
```python
import jax
import jax.numpy as jnp
from jax import lax
from jax.sharding import PartitionSpec as P

HEADS = 16


def passed_along(block, axis, distance):
    devices = range(lax.axis_size(axis))
    route = [(i - distance, i) for i in devices if i - distance in devices]
    return lax.ppermute(block, axis, route)


def layer_norm(values, gain):
    center = values - jnp.mean(values, axis=-1, keepdims=True)
    spread = jnp.mean(center * center, axis=-1, keepdims=True)
    return center * lax.rsqrt(spread + 1e-06) * gain


def body(
    stream,
    queries,
    key_cache,
    value_cache,
    segments,
    stale_rows,
    owners,
    attn_gain,
    w_key,
    key_bias,
    mlp_gain,
    w_fc,
    b_fc,
    w_proj,
    b_proj,
    merge_gain,
    w_merge,
    b_merge,
):
    row_count = stream.shape[0]
    model_width = stream.shape[1]
    head_size = model_width // HEADS
    local_rows = stale_rows % row_count
    held = layer_norm(stream[local_rows].astype(jnp.float32), attn_gain).astype(jnp.bfloat16)
    fresh_keys = (jnp.dot(held, w_key, preferred_element_type=jnp.float32) + key_bias).astype(
        jnp.bfloat16
    )
    refreshed = key_cache.at[local_rows].set(fresh_keys)
    below = passed_along((refreshed, value_cache), "blk", 1)
    above = passed_along((refreshed, value_cache), "blk", -1)
    key_window = jnp.concatenate([below[0], refreshed, above[0]], axis=0).reshape(
        3 * row_count, HEADS, head_size
    )
    value_window = jnp.concatenate([below[1], value_cache, above[1]], axis=0).reshape(
        3 * row_count, HEADS, head_size
    )
    position = lax.axis_index("blk")
    minus_ones = jnp.full((row_count,), -1, jnp.int32)
    seg_padded = jnp.concatenate([minus_ones, segments, minus_ones], axis=0)
    key_seg = lax.dynamic_slice_in_dim(seg_padded, position * row_count, 3 * row_count, 0)
    query_seg = lax.dynamic_slice_in_dim(segments, position * row_count, row_count, 0)
    query_heads = queries.reshape(row_count, HEADS, head_size)
    scores = jnp.einsum(
        "qhd,khd->hqk", query_heads, key_window, preferred_element_type=jnp.float32
    ) * (1.0 / head_size**0.5)
    allowed = (query_seg[:, None] == key_seg[None, :])[None]
    scores = jnp.where(allowed, scores, -jnp.inf)
    top_score = jnp.max(scores, axis=-1, keepdims=True)
    weights = jnp.exp(scores - top_score)
    probs = (weights / jnp.sum(weights, axis=-1, keepdims=True)).astype(jnp.bfloat16)
    attended = jnp.einsum("hqk,khd->qhd", probs, value_window, preferred_element_type=jnp.float32)
    attended = attended.reshape(row_count, model_width).astype(jnp.bfloat16)
    mixed = stream.astype(jnp.float32) + attended.astype(jnp.float32)
    normed = layer_norm(mixed, mlp_gain).astype(jnp.bfloat16)
    group_units = jax.nn.gelu(
        jnp.dot(
            lax.all_gather(normed, "blk", axis=0, tiled=True),
            w_fc,
            preferred_element_type=jnp.float32,
        )
        + b_fc,
        approximate=False,
    ).astype(jnp.bfloat16)
    summed = lax.psum_scatter(
        jnp.dot(group_units, w_proj, preferred_element_type=jnp.float32).astype(jnp.bfloat16),
        "blk",
        scatter_dimension=0,
        tiled=True,
    ).astype(jnp.float32)
    pooled = jnp.mean((mixed + summed).reshape(row_count // 4, 4, model_width), axis=1) + b_proj
    merge_in = layer_norm(pooled, merge_gain).astype(jnp.bfloat16)
    merged = (jnp.dot(merge_in, w_merge, preferred_element_type=jnp.float32) + b_merge).astype(
        jnp.bfloat16
    )
    owner_count = lax.axis_size("tok")
    merged_rows = row_count // 4
    owner_hot = (owners[:, None] == jnp.arange(owner_count, dtype=jnp.int32)[None, :]).astype(
        jnp.int32
    )
    ranking = jnp.sum(jnp.cumsum(owner_hot, axis=0) * owner_hot, axis=-1) - 1
    selector = (
        owners[None, None, :] == jnp.arange(owner_count, dtype=jnp.int32)[:, None, None]
    ) & (ranking[None, None, :] == jnp.arange(merged_rows, dtype=jnp.int32)[None, :, None])
    outgoing = jnp.einsum(
        "osm,md->osd", selector.astype(jnp.bfloat16), merged, preferred_element_type=jnp.float32
    ).astype(jnp.bfloat16)
    arrived = lax.all_to_all(outgoing, "tok", split_axis=0, concat_axis=0, tiled=True)
    delivered = arrived.reshape(1, 1, owner_count * merged_rows, model_width)
    return (refreshed, delivered)


def solution(mesh):
    return jax.shard_map(
        body,
        mesh=mesh,
        in_specs=(
            P(("tok", "blk"), None),
            P(("tok", "blk"), None),
            P(("tok", "blk"), None),
            P(("tok", "blk"), None),
            P("tok"),
            P(("tok", "blk")),
            P(("tok", "blk")),
            P(),
            P(),
            P(),
            P(),
            P(None, "blk"),
            P("blk"),
            P("blk", None),
            P(),
            P(),
            P(),
            P(),
        ),
        out_specs=(P(("tok", "blk"), None), P("tok", "blk", None, None)),
        check_vma=False,
    )
```

profile of v0, /device:TPU:0, one launch (start us, length us, event | category | flops | bytes accessed | tf_op | source)
XLA Modules:
  0.0 274.7 jit_solution(774383592987161788)
XLA Ops:
  7.2 0.0 copy-start
  7.2 0.0 all-gather.2.cloned.1.call-start
  7.3 0.8 compare_select_fusion
  8.1 1.7 gather_fusion
  9.8 0.1 convert_reduce_fusion
  9.9 0.2 fusion.58
  10.1 3.4 %fusion.14 = bf16[12,1664]{1,0:T(8,128)(2,1)S(1)} fusion(bf16[1664,1664]{1,0:T(8,128)(2,1)} %param.26, bf16[12,1664]{1,0:T(8,128)(2,1)S(1)} %gather_fusion, f32[1664]{0:T(1024)} %param.27, f32[1664]{0:T(1024)} %param.25, f32[12]{0:T(128)S(1)} %add_rsqrt_fusion.2, f32[12]{0:T(128)S(1)} %broadcast_multiply_fusion.2), kind=kOutput, calls=%fused_computation.33 | convolution fusion | flops 66593280 | bytes 5631072 | tf_op jit(solution)/shard_map/dot_general | solution.py:46
  13.6 0.9 scatter_fusion
  14.5 0.0 copy-start.2
  14.5 1.3 collective-permute-start.2
  15.9 1.3 collective-permute-start.3
  17.2 5.3 %collective-permute-start = (bf16[128,1664]{1,0:T(8,128)(2,1)S(1)}, bf16[128,1664]{1,0:T(8,128)(2,1)S(1)}, u32[]{:S(2)}, u32[]{:S(2)}) collective-permute-start(bf16[128,1664]{1,0:T(8,128)(2,1)S(1)} %copy-done.5), channel_id=1, source_target_pairs={{0,4},{4,8},{8,12},{12,16},{16,20},{20,24},{24,28},{28,32},{32,36}... | collective-permute-start | bytes 1277960 | tf_op jit(solution)/shard_map/ppermute | solution.py:12
  22.4 1.3 collective-permute-start.1
  23.8 1.0 copy.32
  24.7 0.1 dynamic_slice.6
  24.8 0.1 fusion.82
  24.9 0.1 broadcast_compare_fusion
  25.0 0.0 copy-start.6
  25.1 0.7 copy-done.6
  25.8 1.2 pad_maximum_fusion.1
  27.0 1.5 copy.31
  28.6 1.1 pad_maximum_fusion
  29.7 1.6 copy.30
  31.3 4.4 %fusion.118 = (f32[16,128]{1,0:T(8,128)S(1)}, f32[16,128,384]{1,2,0:T(8,128)}) fusion(pred[128,384]{0,1:T(8,128)(4,1)S(1)} %broadcast_compare_fusion, bf16[384,16,104]{0,2,1:T(8,128)(2,1)} %bitcast.33, bf16[128,16,104]{0,2,1:T(8,128)(2,1)} %bitcast.36), kind=kOutput, calls=%fused_computation.159 | convolution fusion | flops 166723968 | bytes 4907008 | tf_op jit(solution)/shard_map/sub | solution.py:70
  35.7 2.5 fusion.52
  38.2 0.3 copy.34
  38.5 0.0 copy-start.14
  38.6 0.2 fusion.73
  38.7 0.3 multiply_reduce_fusion
  39.0 1.0 multiply_convert_fusion
  40.0 0.0 all-gather.2.cloned.1.call-update
  40.0 0.2 reduce-scatter.2.cloned.1.call-start
  40.2 74.5 %all-gather.2.cloned.1.call-done = bf16[4096,1664]{1,0:T(8,128)(2,1)} async-done(((bf16[128,1664]{1,0:T(8,128)(2,1)}), bf16[4096,1664]{1,0:T(8,128)(2,1)}) %all-gather.2.cloned.1.call-update) | async-done | bytes 13631504 | tf_op jit(solution)/shard_map/all_gather | solution.py:78
  114.7 27.8 %convolution_convert_fusion = bf16[4096,1664]{1,0:T(8,128)(2,1)} fusion(bf16[256,1664]{1,0:T(8,128)(2,1)S(1)} %copy-done, bf16[4096,1664]{1,0:T(8,128)(2,1)} %all-gather.2.cloned.1.call-done, bf16[1664,256]{1,0:T(8,128)(2,1)S(1)} %copy-done.14, f32[256]{0:T(256)S(1)} %copy-done.15), kind=kOutput, calls=%fused_computation.3 | convolution fusion | flops 7055343616 | bytes 28967936 | tf_op jit(solution)/shard_map/dot_general | solution.py:86
  142.6 0.0 reduce-scatter.2.cloned.1.call-update
  142.6 0.6 copy-done.13
  143.2 0.1 fusion.80
  143.3 0.1 reduce_window_sum.11
  143.4 0.2 select_reduce_fusion
  143.6 105.9 %reduce-scatter.2.cloned.1.call-done = bf16[128,1664]{1,0:T(8,128)(2,1)} async-done(((bf16[4096,1664]{1,0:T(8,128)(2,1)}), bf16[128,1664]{1,0:T(8,128)(2,1)}) %reduce-scatter.2.cloned.1.call-update) | async-done | bytes 426000 | tf_op jit(solution)/shard_map/reduce_scatter | solution.py:85
  249.4 1.1 convert_add_fusion
  250.6 0.2 reshape.147
  250.8 0.5 reduce_sum.87
  251.3 0.1 fusion.53
  251.5 0.2 multiply_reduce_fusion.1
  251.7 3.8 %convolution_convert_fusion.1 = bf16[4,32,1664]{2,1,0:T(8,128)(2,1)S(1)} fusion(bf16[1664,1664]{1,0:T(8,128)(2,1)} %param.34, f32[32,1664]{1,0:T(8,128)S(1)} %reduce_sum.87, f32[1664]{0:T(1024)S(1)} %copy-done.11, f32[1664]{0:T(1024)S(1)} %copy-done.12, f32[32]{0:T(128)S(1)} %add_rsqrt_fusion, f32[32]{0:T(128)S(1)} %broadcast_multiply_fusion, ...), kind=kOutput, calls=%fused_computation.27 | convolution fusion | flops 191483904 | bytes 6198144 | tf_op jit(solution)/shard_map/osm,md->osd/dot_general | solution.py:105
  255.5 11.6 %all_to_all.5 = bf16[4,32,1664]{2,1,0:T(8,128)(2,1)S(1)} all-to-all(bf16[4,32,1664]{2,1,0:T(8,128)(2,1)S(1)} %convolution_convert_fusion.1), channel_id=1, replica_groups=mesh['blk'=32,'tok'=4] {'tok'}, dimensions={0} | all-to-all | bytes 851968 | tf_op jit(solution)/shard_map/all_to_all | solution.py:108
  267.1 0.8 copy.40
  (41 shorter events, 0.1 us)
Async XLA Ops:
  7.2 107.6 %copy-start = (bf16[256,1664]{1,0:T(8,128)(2,1)S(1)}, bf16[256,1664]{1,0:T(8,128)(2,1)}, u32[]{:S(2)}) copy-start(bf16[256,1664]{1,0:T(8,128)(2,1)} %param.31) | copy-start | bytes 2555908
  7.2 16.6 %copy-start.7 = (bf16[128,1664]{1,0:T(8,128)(2,1)S(1)}, bf16[128,1664]{1,0:T(8,128)(2,1)}, u32[]{:S(2)}) copy-start(bf16[128,1664]{1,0:T(8,128)(2,1)} %param.19) | copy-start | bytes 1277956
  7.2 6.4 %copy-start.3 = (bf16[128,1664]{1,0:T(8,128)(2,1)S(1)}, bf16[128,1664]{1,0:T(8,128)(2,1)}, u32[]{:S(2)}) copy-start(bf16[128,1664]{1,0:T(8,128)(2,1)} %param.20) | copy-start | bytes 1277956
  7.2 10.0 %copy-start.5 = (bf16[128,1664]{1,0:T(8,128)(2,1)S(1)}, bf16[128,1664]{1,0:T(8,128)(2,1)}, u32[]{:S(2)}) copy-start(bf16[128,1664]{1,0:T(8,128)(2,1)} %param.21) | copy-start | bytes 1277956
  7.2 107.5 %all-gather.2.cloned.1.call-start = ((), (), s32[]{:S(2)}) async-start(), calls=%async_computation.2 | async-start | bytes 14057472 | tf_op jit(solution)/shard_map/all_gather | solution.py:78
  7.3 17.5 %copy-start.9 = (s32[4096]{0:T(1024)S(1)}, s32[4096]{0:T(1024)}, u32[]{:S(2)}) copy-start(s32[4096]{0:T(1024)} %param.22) | copy-start | bytes 49156
  14.5 15.2 %copy-start.2 = (bf16[128,1664]{1,0:T(8,128)(2,1)}, bf16[128,1664]{1,0:T(8,128)(2,1)S(1)}, u32[]{:S(2)}) copy-start(bf16[128,1664]{1,0:T(8,128)(2,1)S(1)} %scatter_fusion) | copy-start | bytes 1277956
  14.5 10.5 %collective-permute-start.2 = (bf16[128,1664]{1,0:T(8,128)(2,1)S(1)}, bf16[128,1664]{1,0:T(8,128)(2,1)S(1)}, u32[]{:S(2)}, u32[]{:S(2)}) collective-permute-start(bf16[128,1664]{1,0:T(8,128)(2,1)S(1)} %scatter_fusion), channel_id=1, source_target_pairs={{0,4},{4,8},{8,12},{12,16},{16,20},{20,24},{24,28},{28,32},{32,36}... | collective-permute-start | bytes 1277960 | tf_op jit(solution)/shard_map/ppermute | solution.py:12
  15.9 9.9 %collective-permute-start.3 = (bf16[128,1664]{1,0:T(8,128)(2,1)S(1)}, bf16[128,1664]{1,0:T(8,128)(2,1)}, u32[]{:S(2)}, u32[]{:S(2)}) collective-permute-start(bf16[128,1664]{1,0:T(8,128)(2,1)S(1)} %scatter_fusion), channel_id=1, source_target_pairs={{4,0},{8,4},{12,8},{16,12},{20,16},{24,20},{28,24},{32,28},{36,32}... | collective-permute-start | bytes 1277960 | tf_op jit(solution)/shard_map/ppermute | solution.py:12
  17.2 11.4 %collective-permute-start = (bf16[128,1664]{1,0:T(8,128)(2,1)S(1)}, bf16[128,1664]{1,0:T(8,128)(2,1)S(1)}, u32[]{:S(2)}, u32[]{:S(2)}) collective-permute-start(bf16[128,1664]{1,0:T(8,128)(2,1)S(1)} %copy-done.5), channel_id=1, source_target_pairs={{0,4},{4,8},{8,12},{12,16},{16,20},{20,24},{24,28},{28,32},{32,36}... | collective-permute-start | bytes 1277960 | tf_op jit(solution)/shard_map/ppermute | solution.py:12
  22.4 6.1 %collective-permute-start.1 = (bf16[128,1664]{1,0:T(8,128)(2,1)S(1)}, bf16[128,1664]{1,0:T(8,128)(2,1)}, u32[]{:S(2)}, u32[]{:S(2)}) collective-permute-start(bf16[128,1664]{1,0:T(8,128)(2,1)S(1)} %copy-done.5), channel_id=1, source_target_pairs={{4,0},{8,4},{12,8},{16,12},{20,16},{24,20},{28,24},{32,28},{36,32}... | collective-permute-start | bytes 1277960 | tf_op jit(solution)/shard_map/ppermute | solution.py:12
  25.0 0.8 copy-start.6
  31.3 4.4 %copy-start.4 = (bf16[384,1664]{0,1:T(8,128)(2,1)S(1)}, bf16[384,1664]{0,1:T(8,128)(2,1)}, u32[]{:S(2)}) copy-start(bf16[384,1664]{0,1:T(8,128)(2,1)} %copy.30) | copy-start | bytes 3833860
  35.7 2.9 %copy-start.1 = (bf16[128,1664]{1,0:T(8,128)(2,1)S(1)}, bf16[128,1664]{1,0:T(8,128)(2,1)}, u32[]{:S(2)}) copy-start(bf16[128,1664]{1,0:T(8,128)(2,1)} %param.18) | copy-start | bytes 1277956
  38.2 0.8 copy-start.10
  38.2 76.5 %copy-start.15 = (f32[256]{0:T(256)S(1)}, f32[256]{0:T(256)}, u32[]{:S(2)}) copy-start(f32[256]{0:T(256)} %param.30) | copy-start | bytes 3076
  38.5 76.2 %copy-start.14 = (bf16[1664,256]{1,0:T(8,128)(2,1)S(1)}, bf16[1664,256]{1,0:T(8,128)(2,1)}, u32[]{:S(2)}) copy-start(bf16[1664,256]{1,0:T(8,128)(2,1)} %param.29) | copy-start | bytes 2555908
  40.0 209.4 %reduce-scatter.2.cloned.1.call-start = ((), (), s32[]{:S(2)}) async-start(), calls=%async_computation.3 | async-start | bytes 14057472 | tf_op jit(solution)/shard_map/reduce_scatter | solution.py:85
  142.6 0.7 copy-start.13
  143.2 108.1 %copy-start.8 = (f32[1664]{0:T(1024)S(1)}, f32[1664]{0:T(1024)}, u32[]{:S(2)}) copy-start(f32[1664]{0:T(1024)} %param.32) | copy-start | bytes 19972
  143.2 108.5 %copy-start.11 = (f32[1664]{0:T(1024)S(1)}, f32[1664]{0:T(1024)}, u32[]{:S(2)}) copy-start(f32[1664]{0:T(1024)} %param.35) | copy-start | bytes 19972
  143.2 108.5 %copy-start.12 = (f32[1664]{0:T(1024)S(1)}, f32[1664]{0:T(1024)}, u32[]{:S(2)}) copy-start(f32[1664]{0:T(1024)} %param.33) | copy-start | bytes 19972
Sparse Core Ops, SparseCore 0:
  40.1 74.5 all-gather.1
  142.7 106.6 reduce-scatter.1
where the time goes:
time: 275 us
  waiting for transfers between devices  180 us (65%)
  matrix products  42 us (15%)
  between operations  14.3 us (5%)
  blocking collectives  11.6 us (4%)
  local copies, waits for them, and re-layouts  9.54 us (3%)
  starting transfers between devices  9.43 us (3%)
  other arithmetic  7.38 us (3%)
    reduce_scatter x1, waiting for transfers between devices, body(): lax.psum_scatter(jnp.dot(group_units, w_proj, preferred_element_type=jnp....  106 us
    all_gather x1, waiting for transfers between devices, body(): lax.all_gather(normed, 'blk', axis=0, tiled=True)  74.5 us
    dot_general x1, matrix products, body(): jnp.dot(group_units, w_proj, preferred_element_type=jnp.float32)  27.8 us
    all_to_all x1, blocking collectives, body(): lax.all_to_all(outgoing, 'tok', split_axis=0, concat_axis=0, tiled=True)  11.6 us
    ppermute x4, starting transfers between devices, passed_along(): return lax.ppermute(block, axis, route)  9.17 us
  transfers between devices with their start and end apart: 6, of which 2 were waited for; matrix products, arithmetic and copies ran while one was open for 2% of the time, Pallas kernels for 0%

commit v1 on v0

--- a/solution.py
+++ b/solution.py
@@ -75,7 +75,9 @@
     normed = layer_norm(mixed, mlp_gain).astype(jnp.bfloat16)
     group_units = jax.nn.gelu(
         jnp.dot(
-            lax.all_gather(normed, "blk", axis=0, tiled=True),
+            jnp.concatenate(
+                lax.all_to_all(jnp.stack([normed] * lax.axis_size("blk")), "blk", 0, 0), axis=0
+            ),
             w_fc,
             preferred_element_type=jnp.float32,
         )

time: 275 us -> 372 us (1.35)
  blocking collectives: 11.6 us -> 179 us
  waiting for transfers between devices: 180 us -> 105 us
  local copies, waits for them, and re-layouts: 9.54 us -> 16.1 us
    all_to_all x0 -> x1, blocking collectives: none -> 167 us  [body(): lax.all_to_all(jnp.stack([normed] * lax.axis_size('blk')), 'blk', 0, 0)]
    all_gather x1 -> x0, waiting for transfers between devices: 74.5 us -> none  [body(): lax.all_gather(normed, 'blk', axis=0, tiled=True)]
    another operation x0 -> x1, local copies, waits for them, and re-layouts: none -> 6.59 us  [body(): jnp.stack([normed] * lax.axis_size('blk'))]
  transfers between devices with their start and end apart: 6 -> 5, of which waited for: 2 -> 1; matrix products, arithmetic and copies ran while one was open for 2% -> 1% of each run, Pallas kernels for 0% -> 0%
where the time goes in v1:
time: 372 us
  blocking collectives  179 us (48%)
  waiting for transfers between devices  105 us (28%)
  matrix products  42 us (11%)
  local copies, waits for them, and re-layouts  16.1 us (4%)
  between operations  14.3 us (4%)
  starting transfers between devices  9.21 us (2%)
  other arithmetic  6.62 us (2%)
    all_to_all x1, blocking collectives, body(): lax.all_to_all(jnp.stack([normed] * lax.axis_size('blk')), 'blk', 0, 0)  167 us
    reduce_scatter x1, waiting for transfers between devices, body(): lax.psum_scatter(jnp.dot(group_units, w_proj, preferred_element_type=jnp....  105 us
    dot_general x1, matrix products, body(): jnp.dot(group_units, w_proj, preferred_element_type=jnp.float32)  27.8 us
    all_to_all x1, blocking collectives, body(): lax.all_to_all(outgoing, 'tok', split_axis=0, concat_axis=0, tiled=True)  11.6 us
    ppermute x4, starting transfers between devices, passed_along(): return lax.ppermute(block, axis, route)  9.17 us
  transfers between devices with their start and end apart: 5, of which 1 were waited for; matrix products, arithmetic and copies ran while one was open for 1% of the time, Pallas kernels for 0%

profile of v1, /device:TPU:0, one launch (start us, length us, event | category | flops | bytes accessed | tf_op | source)
XLA Modules:
  0.0 371.5 jit_solution(14682407387627105649)
XLA Ops:
  7.2 0.0 copy-start
  7.2 0.0 reduce-scatter.2.cloned.1.call-start
  7.3 0.8 compare_select_fusion
  8.1 1.7 gather_fusion
  9.8 0.1 convert_reduce_fusion
  9.9 0.2 fusion.58
  10.1 3.4 fusion.14
  13.6 0.9 scatter_fusion
  14.5 0.0 copy-start.3
  14.5 1.3 collective-permute-start.2
  15.9 1.3 collective-permute-start.3
  17.2 5.3 %collective-permute-start = (bf16[128,1664]{1,0:T(8,128)(2,1)S(1)}, bf16[128,1664]{1,0:T(8,128)(2,1)S(1)}, u32[]{:S(2)}, u32[]{:S(2)}) collective-permute-start(bf16[128,1664]{1,0:T(8,128)(2,1)S(1)} %copy-done.6), channel_id=1, source_target_pairs={{0,4},{4,8},{8,12},{12,16},{16,20},{20,24},{24,28},{28,32},{32,36}... | collective-permute-start | bytes 1277960 | tf_op jit(solution)/shard_map/ppermute | solution.py:12
  22.4 1.3 collective-permute-start.1
  23.8 1.0 copy.32
  24.7 0.1 dynamic_slice.6
  24.8 0.1 fusion.82
  24.9 0.1 broadcast_compare_fusion
  25.0 0.0 copy-start.7
  25.1 0.7 copy-done.7
  25.8 1.2 pad_maximum_fusion.1
  27.0 1.5 copy.31
  28.6 1.1 pad_maximum_fusion
  29.7 1.6 copy.30
  31.3 4.4 %fusion.118 = (f32[16,128]{1,0:T(8,128)S(1)}, f32[16,128,384]{1,2,0:T(8,128)}) fusion(pred[128,384]{0,1:T(8,128)(4,1)S(1)} %broadcast_compare_fusion, bf16[384,16,104]{0,2,1:T(8,128)(2,1)} %bitcast.35, bf16[128,16,104]{0,2,1:T(8,128)(2,1)} %bitcast.38), kind=kOutput, calls=%fused_computation.159 | convolution fusion | flops 166723968 | bytes 4907008 | tf_op jit(solution)/shard_map/sub | solution.py:70
  35.7 2.5 fusion.52
  38.2 0.0 copy-start.11
  38.2 0.3 copy.34
  38.5 0.2 fusion.73
  38.7 0.3 multiply_reduce_fusion
  39.0 0.2 multiply_convert_fusion
  39.2 6.6 %stack.2 = bf16[32,128,1664]{2,1,0:T(8,128)(2,1)} broadcast(bf16[128,1664]{1,0:T(8,128)(2,1)S(1)} %multiply_convert_fusion), dimensions={1,2} | broadcast | bytes 14057472 | tf_op jit(solution)/shard_map/stack | solution.py:79
  45.8 166.9 %all_to_all.10 = bf16[32,128,1664]{2,1,0:T(8,128)(2,1)} all-to-all(bf16[32,128,1664]{2,1,0:T(8,128)(2,1)} %stack.2), channel_id=1, replica_groups=mesh['blk'=32,'tok'=4] {'blk'}, dimensions={0} | all-to-all | bytes 27262976 | tf_op jit(solution)/shard_map/all_to_all | solution.py:79
  212.7 27.8 %convolution_convert_fusion = bf16[4096,1664]{1,0:T(8,128)(2,1)} fusion(bf16[256,1664]{1,0:T(8,128)(2,1)S(1)} %copy-done, bf16[4096,1664]{1,0:T(8,128)(2,1)} %bitcast.33, bf16[1664,256]{1,0:T(8,128)(2,1)S(1)} %copy-done.15, f32[256]{0:T(256)S(1)} %copy-done.16), kind=kOutput, calls=%fused_computation.3 | convolution fusion | flops 7055343616 | bytes 28967936 | tf_op jit(solution)/shard_map/dot_general | solution.py:88
  240.5 0.0 reduce-scatter.2.cloned.1.call-update
  240.5 0.6 copy-done.14
  241.1 0.1 fusion.80
  241.2 0.1 reduce_window_sum.11
  241.3 0.2 select_reduce_fusion
  241.5 104.7 %reduce-scatter.2.cloned.1.call-done = bf16[128,1664]{1,0:T(8,128)(2,1)} async-done(((bf16[4096,1664]{1,0:T(8,128)(2,1)}), bf16[128,1664]{1,0:T(8,128)(2,1)}) %reduce-scatter.2.cloned.1.call-update) | async-done | bytes 426000 | tf_op jit(solution)/shard_map/reduce_scatter | solution.py:87
  346.2 1.1 convert_add_fusion
  347.3 0.2 reshape.153
  347.6 0.0 copy-start.1
  347.6 0.5 reduce_sum.87
  348.1 0.1 fusion.53
  348.2 0.2 multiply_reduce_fusion.1
  348.5 3.8 %convolution_convert_fusion.1 = bf16[4,32,1664]{2,1,0:T(8,128)(2,1)S(1)} fusion(bf16[1664,1664]{1,0:T(8,128)(2,1)} %param.34, f32[32,1664]{1,0:T(8,128)S(1)} %reduce_sum.87, f32[1664]{0:T(1024)S(1)} %copy-done.12, f32[1664]{0:T(1024)S(1)} %copy-done.13, f32[32]{0:T(128)S(1)} %add_rsqrt_fusion, f32[32]{0:T(128)S(1)} %broadcast_multiply_fusion, ...), kind=kOutput, calls=%fused_computation.27 | convolution fusion | flops 191483904 | bytes 6198144 | tf_op jit(solution)/shard_map/osm,md->osd/dot_general | solution.py:107
  352.3 11.6 %all_to_all.11 = bf16[4,32,1664]{2,1,0:T(8,128)(2,1)S(1)} all-to-all(bf16[4,32,1664]{2,1,0:T(8,128)(2,1)S(1)} %convolution_convert_fusion.1), channel_id=1, replica_groups=mesh['blk'=32,'tok'=4] {'tok'}, dimensions={0} | all-to-all | bytes 851968 | tf_op jit(solution)/shard_map/all_to_all | solution.py:110
  363.9 0.8 copy.40
  (42 shorter events, 0.1 us)
Async XLA Ops:
  7.2 205.5 %copy-start = (bf16[256,1664]{1,0:T(8,128)(2,1)S(1)}, bf16[256,1664]{1,0:T(8,128)(2,1)}, u32[]{:S(2)}) copy-start(bf16[256,1664]{1,0:T(8,128)(2,1)} %param.31) | copy-start | bytes 2555908
  7.2 16.6 %copy-start.8 = (bf16[128,1664]{1,0:T(8,128)(2,1)S(1)}, bf16[128,1664]{1,0:T(8,128)(2,1)}, u32[]{:S(2)}) copy-start(bf16[128,1664]{1,0:T(8,128)(2,1)} %param.19) | copy-start | bytes 1277956
  7.2 6.4 %copy-start.4 = (bf16[128,1664]{1,0:T(8,128)(2,1)S(1)}, bf16[128,1664]{1,0:T(8,128)(2,1)}, u32[]{:S(2)}) copy-start(bf16[128,1664]{1,0:T(8,128)(2,1)} %param.20) | copy-start | bytes 1277956
  7.2 10.0 %copy-start.6 = (bf16[128,1664]{1,0:T(8,128)(2,1)S(1)}, bf16[128,1664]{1,0:T(8,128)(2,1)}, u32[]{:S(2)}) copy-start(bf16[128,1664]{1,0:T(8,128)(2,1)} %param.21) | copy-start | bytes 1277956
  7.2 339.0 %reduce-scatter.2.cloned.1.call-start = ((), (), s32[]{:S(2)}) async-start(), calls=%async_computation.3 | async-start | bytes 14057472 | tf_op jit(solution)/shard_map/reduce_scatter | solution.py:87
  7.3 17.5 %copy-start.10 = (s32[4096]{0:T(1024)S(1)}, s32[4096]{0:T(1024)}, u32[]{:S(2)}) copy-start(s32[4096]{0:T(1024)} %param.22) | copy-start | bytes 49156
  14.5 15.2 %copy-start.3 = (bf16[128,1664]{1,0:T(8,128)(2,1)}, bf16[128,1664]{1,0:T(8,128)(2,1)S(1)}, u32[]{:S(2)}) copy-start(bf16[128,1664]{1,0:T(8,128)(2,1)S(1)} %scatter_fusion) | copy-start | bytes 1277956
  14.5 10.5 %collective-permute-start.2 = (bf16[128,1664]{1,0:T(8,128)(2,1)S(1)}, bf16[128,1664]{1,0:T(8,128)(2,1)S(1)}, u32[]{:S(2)}, u32[]{:S(2)}) collective-permute-start(bf16[128,1664]{1,0:T(8,128)(2,1)S(1)} %scatter_fusion), channel_id=1, source_target_pairs={{0,4},{4,8},{8,12},{12,16},{16,20},{20,24},{24,28},{28,32},{32,36}... | collective-permute-start | bytes 1277960 | tf_op jit(solution)/shard_map/ppermute | solution.py:12
  15.9 9.9 %collective-permute-start.3 = (bf16[128,1664]{1,0:T(8,128)(2,1)S(1)}, bf16[128,1664]{1,0:T(8,128)(2,1)}, u32[]{:S(2)}, u32[]{:S(2)}) collective-permute-start(bf16[128,1664]{1,0:T(8,128)(2,1)S(1)} %scatter_fusion), channel_id=1, source_target_pairs={{4,0},{8,4},{12,8},{16,12},{20,16},{24,20},{28,24},{32,28},{36,32}... | collective-permute-start | bytes 1277960 | tf_op jit(solution)/shard_map/ppermute | solution.py:12
  17.2 11.4 %collective-permute-start = (bf16[128,1664]{1,0:T(8,128)(2,1)S(1)}, bf16[128,1664]{1,0:T(8,128)(2,1)S(1)}, u32[]{:S(2)}, u32[]{:S(2)}) collective-permute-start(bf16[128,1664]{1,0:T(8,128)(2,1)S(1)} %copy-done.6), channel_id=1, source_target_pairs={{0,4},{4,8},{8,12},{12,16},{16,20},{20,24},{24,28},{28,32},{32,36}... | collective-permute-start | bytes 1277960 | tf_op jit(solution)/shard_map/ppermute | solution.py:12
  22.4 6.1 %collective-permute-start.1 = (bf16[128,1664]{1,0:T(8,128)(2,1)S(1)}, bf16[128,1664]{1,0:T(8,128)(2,1)}, u32[]{:S(2)}, u32[]{:S(2)}) collective-permute-start(bf16[128,1664]{1,0:T(8,128)(2,1)S(1)} %copy-done.6), channel_id=1, source_target_pairs={{4,0},{8,4},{12,8},{16,12},{20,16},{24,20},{28,24},{32,28},{36,32}... | collective-permute-start | bytes 1277960 | tf_op jit(solution)/shard_map/ppermute | solution.py:12
  25.0 0.8 copy-start.7
  31.3 4.4 %copy-start.5 = (bf16[384,1664]{0,1:T(8,128)(2,1)S(1)}, bf16[384,1664]{0,1:T(8,128)(2,1)}, u32[]{:S(2)}) copy-start(bf16[384,1664]{0,1:T(8,128)(2,1)} %copy.30) | copy-start | bytes 3833860
  35.7 2.9 copy-start.2
  38.2 0.8 copy-start.11
  45.8 166.9 %copy-start.15 = (bf16[1664,256]{1,0:T(8,128)(2,1)S(1)}, bf16[1664,256]{1,0:T(8,128)(2,1)}, u32[]{:S(2)}) copy-start(bf16[1664,256]{1,0:T(8,128)(2,1)} %param.29) | copy-start | bytes 2555908
  45.8 166.9 %copy-start.16 = (f32[256]{0:T(256)S(1)}, f32[256]{0:T(256)}, u32[]{:S(2)}) copy-start(f32[256]{0:T(256)} %param.30) | copy-start | bytes 3076
  240.5 0.7 copy-start.14
  241.1 106.9 %copy-start.9 = (f32[1664]{0:T(1024)S(1)}, f32[1664]{0:T(1024)}, u32[]{:S(2)}) copy-start(f32[1664]{0:T(1024)} %param.32) | copy-start | bytes 19972
  241.1 107.3 %copy-start.12 = (f32[1664]{0:T(1024)S(1)}, f32[1664]{0:T(1024)}, u32[]{:S(2)}) copy-start(f32[1664]{0:T(1024)} %param.35) | copy-start | bytes 19972
  241.1 107.3 %copy-start.13 = (f32[1664]{0:T(1024)S(1)}, f32[1664]{0:T(1024)}, u32[]{:S(2)}) copy-start(f32[1664]{0:T(1024)} %param.33) | copy-start | bytes 19972
  347.6 17.1 %copy-start.1 = (bf16[256,1664]{1,0:T(8,128)(2,1)S(1)}, bf16[256,1664]{1,0:T(8,128)(2,1)}, u32[]{:S(2)}) copy-start(bf16[256,1664]{1,0:T(8,128)(2,1)} %param.31) | copy-start | bytes 2555908
Sparse Core Ops, SparseCore 0:
  240.6 105.4 reduce-scatter.1
